TPU v7x, 256 devices: a whole 4x4x8 slice. The times are simulated.
256 devices in a mesh: freq: 16 (over x, z_hi), tmpl: 16 (over y, z_lo, core).
Axes of the slice: x: 4, y: 4, z: 8 (z_hi: 4, z_lo: 2; z = z_hi * 2 + z_lo), core: 2. Of those that a mesh axis runs over, the one named last changes fastest.
Arguments:
- strain_spectrum: float32 [2, 1024, 1024], P(None, 'freq', 'tmpl'), may hold values from -6 to 6
- bank_spectra: bfloat16 [128, 2, 1024, 1024], P('tmpl', None, 'freq'), may hold values from -0.0029296875 to 0.0029296875
Outputs:
- snr_peaks: float32 [128, 1048576], P('tmpl', 'freq')
All inputs are finite; a program needn't handle non-finite values.
Results may differ from a plain program's by a relative error of at most 0.0031.
Values may be sent and summed in bfloat16 or wider, within the bound.
A program may use at most 64 MiB of HBM per device.

v0:
```python
import math

import jax
import jax.numpy as jnp
from jax import lax
from jax.sharding import PartitionSpec as P

WIN = 256


def with_halo(cells, sides, width):
    for axis, dim in sides:
        count = lax.axis_size(axis)
        head = lax.slice_in_dim(cells, 0, width, axis=dim)
        tail = lax.slice_in_dim(cells, cells.shape[dim] - width, cells.shape[dim], axis=dim)
        cells = jnp.concatenate(
            [
                lax.ppermute(tail, axis, [(i, (i + 1) % count) for i in range(count)]),
                cells,
                lax.ppermute(head, axis, [((i + 1) % count, i) for i in range(count)]),
            ],
            axis=dim,
        )
    return cells


def circle(length):
    ramp_index = jnp.arange(length, dtype=jnp.int32)
    angles = (ramp_index[:, None] * ramp_index[None, :] % length).astype(jnp.float32) * (
        2.0 * math.pi / length
    )
    return (jnp.cos(angles), jnp.sin(angles))


def rotation(length):
    cosine_table, sine_table = circle(length)
    top_half = jnp.concatenate([cosine_table, sine_table], axis=1)
    low_half = jnp.concatenate([-sine_table, cosine_table], axis=1)
    return jnp.concatenate([top_half, low_half], axis=0).astype(jnp.bfloat16)


def twiddle(first_row, row_count, columns, period):
    row_index = first_row + jnp.arange(row_count, dtype=jnp.int32)
    ramp_index = jnp.arange(columns, dtype=jnp.int32)
    angles = (row_index[:, None] * ramp_index[None, :]).astype(jnp.float32) * (
        2.0 * math.pi / period
    )
    return (jnp.cos(angles), jnp.sin(angles))


def sliding(padded, window):
    current = padded
    covered = 1
    while covered < window:
        stride = min(covered, window - covered)
        current = jnp.maximum(current[..., :-stride], current[..., stride:])
        covered = covered + stride
    return current


def shards(strain_spectrum, bank_spectra):
    template_count = bank_spectra.shape[0]
    rows_here = bank_spectra.shape[2]
    columns = bank_spectra.shape[3]
    groups = lax.axis_size("freq")
    transform_rows = rows_here * groups
    local_columns = columns // groups
    height = transform_rows // groups
    window_radius = WIN // 2
    strain = lax.all_gather(strain_spectrum, "tmpl", axis=2, tiled=True)
    spectrum = bank_spectra.astype(jnp.float32)
    real_part = strain[0] * spectrum[:, 0] + strain[1] * spectrum[:, 1]
    imag_part = strain[1] * spectrum[:, 0] - strain[0] * spectrum[:, 1]
    cross_spectrum = jnp.concatenate([real_part, imag_part], axis=2).astype(jnp.bfloat16)
    forward_transform = rotation(columns)
    initial_transform = jnp.einsum(
        "ulw,wj->ulj", cross_spectrum, forward_transform, preferred_element_type=jnp.float32
    )
    cosine_turn, sine_rotation = twiddle(
        lax.axis_index("freq") * rows_here, rows_here, columns, transform_rows * columns
    )
    first_real = initial_transform[..., :columns]
    first_imag = initial_transform[..., columns:]
    rotated_real = first_real * cosine_turn - first_imag * sine_rotation
    turned_imag = first_real * sine_rotation + first_imag * cosine_turn
    stacked = jnp.stack([rotated_real, turned_imag], axis=1).astype(jnp.bfloat16)
    backward = rotation(transform_rows).reshape(2, groups, rows_here, 2 * transform_rows)
    received = lax.all_to_all(stacked, "freq", split_axis=3, concat_axis=3, tiled=True)
    shaped = received.reshape(received.shape[0], 2, rows_here, groups, local_columns)
    second_pass = jnp.einsum(
        "tcasb,csad->tbd", shaped, backward, preferred_element_type=jnp.float32
    )
    energy = second_pass[..., :transform_rows] ** 2 + second_pass[..., transform_rows:] ** 2
    arrived = lax.all_to_all(energy, "freq", split_axis=2, concat_axis=2, tiled=True)
    series = arrived.reshape(template_count, local_columns, groups, height).transpose(0, 3, 2, 1)
    series = series.reshape(template_count, height * columns)
    padded = with_halo(series, (("freq", 1),), window_radius)
    return sliding(padded, WIN)[:, : height * columns]


def solution(mesh):
    in_specs = (P(None, "freq", "tmpl"), P("tmpl", None, "freq", None))
    out_specs = P("tmpl", "freq")
    return jax.shard_map(shards, mesh=mesh, in_specs=in_specs, out_specs=out_specs, check_vma=False)
```

profile of v0, /device:TPU:1, one launch (start us, length us, event | category | flops | bytes accessed | tf_op | source)
XLA Modules:
  0.0 267.1 jit_solution(4096767753524538024)
XLA Ops:
  0.0 0.0 copy-start.2
  0.0 17.6 %fusion.17 = (bf16[1024,1024]{1,0:T(8,128)(2,1)S(1)}, bf16[1024,1024]{1,0:T(8,128)(2,1)}) fusion(), kind=kLoop, calls=%fused_computation.35 | loop fusion | flops 16777216 | bytes 4194304 | tf_op jit(solution)/shard_map/sin | solution.py:32
  17.6 16.5 %fusion.19 = bf16[1024,1024]{1,0:T(8,128)(2,1)} fusion(), kind=kLoop, calls=%fused_computation.39 | loop fusion | flops 16777216 | bytes 2097152 | tf_op jit(solution)/shard_map/neg | solution.py:38
  34.2 0.0 copy-done.2
  34.2 0.1 copy.6
  34.3 27.4 %all_gather.3 = f32[2,64,1024]{1,0,2:T(2,128)S(1)} all-gather(f32[2,64,64]{1,0,2:T(2,128)S(1)} %copy.6), channel_id=1, replica_groups=mesh['freq'=16,'tmpl'=16] {'tmpl'}, dimensions={2}, use_global_device_ids=true | all-gather | bytes 557056 | tf_op jit(solution)/shard_map/all_gather | solution.py:70
  61.7 0.8 fusion.27
  62.5 0.2 copy.7
  62.7 0.2 copy.9
  62.8 4.0 %copy_convert_fusion = f32[8,2,64,1024]{3,2,0,1:T(8,128)} fusion(bf16[8,2,64,1024]{3,2,1,0:T(8,128)(2,1)} %param.3), kind=kLoop, calls=%fused_computation.32 | loop fusion | flops 1048576 | bytes 6291456 | tf_op jit(solution)/shard_map/convert_element_type | solution.py:71
  66.9 1.0 fusion.23
  67.9 0.0 copy-start
  67.9 16.0 %maximum_convert_fusion = bf16[2048,2048]{1,0:T(8,128)(2,1)S(1)} fusion(bf16[1024,1024]{1,0:T(8,128)(2,1)} %get-tuple-element.18, bf16[1024,1024]{1,0:T(8,128)(2,1)} %fusion.19, bf16[1024,1024]{1,0:T(8,128)(2,1)S(1)} %get-tuple-element.17), kind=kLoop, calls=%fused_computation | loop fusion | flops 33554432 | bytes 14680064 | tf_op jit(solution)/shard_map/convert_element_type | solution.py:39
  83.9 0.0 copy-done
  83.9 0.0 copy-start.1
  83.9 0.7 add_convert_fusion.1
  84.7 4.6 %fusion = f32[8,64,2048]{2,1,0:T(8,128)S(1)} fusion(bf16[2048,2048]{1,0:T(8,128)(2,1)S(1)} %maximum_convert_fusion, bf16[8,64,1024]{2,1,0:T(8,128)(2,1)S(1)} %get-tuple-element.8, bf16[8,64,1024]{2,1,0:T(8,128)(2,1)S(1)} %get-tuple-element.7), kind=kOutput, calls=%fused_computation.1 | convolution fusion | flops 4299161600 | bytes 14680064 | tf_op jit(solution)/shard_map/ulw,wj->ulj/dot_general | solution.py:76
  89.2 0.0 copy-done.1
  89.2 0.7 fusion.20
  90.0 0.2 pad_maximum_fusion
  90.2 4.9 %copy.10 = bf16[8,2,64,1024]{2,0,1,3:T(8,128)(2,1)} copy(bf16[8,2,64,1024]{3,2,0,1:T(8,128)(2,1)S(1)} %pad_maximum_fusion) | data formatting | bytes 4194304 | tf_op jit(solution)/shard_map/stack | solution.py:86
  95.1 6.3 %reshape.62 = bf16[16,2,32768]{2,1,0:T(2,128)(2,1)S(1)} reshape(bf16[1024,2,8,64]{3,2,1,0:T(8,128)(2,1)} %bitcast.41) | data formatting | bytes 4194304
  101.5 59.2 %all_to_all.10 = bf16[16,2,32768]{2,1,0:T(2,128)(2,1)} all-to-all(bf16[16,2,32768]{2,1,0:T(2,128)(2,1)S(1)} %reshape.62), channel_id=1, replica_groups=mesh['freq'=16,'tmpl'=16] {'freq'}, dimensions={0} | all-to-all | bytes 4194304 | tf_op jit(solution)/shard_map/all_to_all | solution.py:88
  160.6 7.4 %reshape.63 = bf16[1024,2,8,64]{3,2,1,0:T(8,128)(2,1)} reshape(bf16[16,2,32768]{2,1,0:T(2,128)(2,1)} %all_to_all.10) | data formatting | bytes 4194304
  168.1 8.3 %fusion.10 = f32[8,64,2048]{2,1,0:T(8,128)S(1)} fusion(bf16[2,16,64,2048,1]{3,2,1,4,0:T(8,128)(2,1)} %bitcast.44, bf16[8,2,64,16,64]{2,0,1,4,3:T(8,128)(2,1)} %bitcast.45), kind=kOutput, calls=%fused_computation.14 | convolution fusion | flops 4294967296 | bytes 14680064 | tf_op jit(solution)/shard_map/tcasb,csad->tbd/dot_general | solution.py:90
  176.4 0.4 fusion.13
  176.9 2.8 %copy.12 = f32[8,64,1024]{1,0,2:T(8,128)} copy(f32[8,64,1024]{2,1,0:T(8,128)S(1)} %fusion.13) | data formatting | bytes 4194304 | tf_op jit(solution)/shard_map/add | solution.py:93
  179.6 4.5 %reshape.64 = f32[16,1,32768]{2,1,0:T(1,128)S(1)} reshape(f32[1024,8,64]{2,1,0:T(8,128)} %bitcast.42) | data formatting | bytes 4194304
  184.2 49.0 %all_to_all.11 = f32[16,1,32768]{2,1,0:T(1,128)} all-to-all(f32[16,1,32768]{2,1,0:T(1,128)S(1)} %reshape.64), channel_id=1, replica_groups=mesh['freq'=16,'tmpl'=16] {'freq'}, dimensions={0} | all-to-all | bytes 4194304 | tf_op jit(solution)/shard_map/all_to_all | solution.py:94
  233.2 0.5 broadcast.56
  233.7 7.3 %reduce = f32[16,32768]{1,0:T(8,128)S(1)} reduce(f32[16,1,32768]{2,1,0:T(1,128)} %all_to_all.11, f32[]{:T(128)} %broadcast.56), dimensions={1}, to_apply=%all_to_all.7.reduce_sub_computation | reduce | bytes 4194308 | tf_op jit(solution)/shard_map/all_to_all | solution.py:94
  241.0 3.0 %reshape.65 = f32[1024,8,64]{2,1,0:T(8,128)} reshape(f32[16,32768]{1,0:T(8,128)S(1)} %reduce) | data formatting | bytes 4194304
  244.0 6.6 %copy.13 = f32[8,64,16,64]{3,2,1,0:T(8,128)} copy(f32[8,64,16,64]{3,0,1,2:T(8,128)} %bitcast.43) | data formatting | bytes 4194304 | tf_op jit(solution)/shard_map/transpose | solution.py:95
  250.6 3.4 %reshape.58 = f32[8,65536]{1,0:T(8,128)S(1)} reshape(f32[8,64,16,64]{3,2,1,0:T(8,128)} %copy.13) | data formatting | bytes 4194304 | tf_op jit(solution)/shard_map/reshape | solution.py:96
  254.0 3.3 %collective-permute-start = (f32[8,128]{1,0:T(8,128)S(1)}, f32[8,128]{1,0:T(8,128)S(1)}, u32[]{:S(2)}, u32[]{:S(2)}) collective-permute-start(f32[8,128]{1,0:T(8,128)S(1)} %get-tuple-element.12), channel_id=1, source_target_pairs={{0,16},{16,32},{32,48},{48,64},{64,80},{80,96},{96,112},{112,128},... | collective-permute-start | bytes 12296 | tf_op jit(solution)/shard_map/ppermute | solution.py:18
  257.3 2.5 collective-permute-start.1
  259.8 1.0 collective-permute-done
  260.8 0.1 constant_dynamic-update-slice_fusion.1
  260.9 0.0 collective-permute-done.1
  260.9 0.6 slice_maximum_fusion.6
  261.6 0.6 slice_maximum_fusion.5
  262.2 0.6 slice_maximum_fusion.4
  262.8 0.6 slice_maximum_fusion.3
  263.4 0.6 slice_maximum_fusion.2
  264.0 0.6 slice_maximum_fusion.1
  264.6 0.6 slice_maximum_fusion
  265.2 0.3 fusion.25
  265.5 1.6 slice_maximum_fusion.7
  (4 shorter events, 0.0 us)
Async XLA Ops:
  0.0 34.2 %copy-start.2 = (f32[2,64,64]{2,1,0:T(8,128)S(1)}, f32[2,64,64]{2,1,0:T(8,128)}, u32[]{:S(2)}) copy-start(f32[2,64,64]{2,1,0:T(8,128)} %param.2) | copy-start | bytes 98308
  67.9 16.0 %copy-start = (f32[8,2,64,1024]{3,2,0,1:T(8,128)S(1)}, f32[8,2,64,1024]{3,2,0,1:T(8,128)}, u32[]{:S(2)}) copy-start(f32[8,2,64,1024]{3,2,0,1:T(8,128)} %copy_convert_fusion) | copy-start | bytes 12582916
  83.9 5.3 %copy-start.1 = (bf16[2048,2048]{1,0:T(8,128)(2,1)}, bf16[2048,2048]{1,0:T(8,128)(2,1)S(1)}, u32[]{:S(2)}) copy-start(bf16[2048,2048]{1,0:T(8,128)(2,1)S(1)} %maximum_convert_fusion) | copy-start | bytes 25165828
  254.0 6.8 %collective-permute-start = (f32[8,128]{1,0:T(8,128)S(1)}, f32[8,128]{1,0:T(8,128)S(1)}, u32[]{:S(2)}, u32[]{:S(2)}) collective-permute-start(f32[8,128]{1,0:T(8,128)S(1)} %get-tuple-element.12), channel_id=1, source_target_pairs={{0,16},{16,32},{32,48},{48,64},{64,80},{80,96},{96,112},{112,128},... | collective-permute-start | bytes 12296 | tf_op jit(solution)/shard_map/ppermute | solution.py:18
  257.3 3.6 %collective-permute-start.1 = (f32[8,128]{1,0:T(8,128)S(1)}, f32[8,128]{1,0:T(8,128)S(1)}, u32[]{:S(2)}, u32[]{:S(2)}) collective-permute-start(f32[8,128]{1,0:T(8,128)S(1)} %get-tuple-element.11), channel_id=1, source_target_pairs={{16,0},{32,16},{48,32},{64,48},{80,64},{96,80},{112,96},{128,112},... | collective-permute-start | bytes 12296 | tf_op jit(solution)/shard_map/ppermute | solution.py:20
where the time goes:
time: 269 us; the launch traced here: 267 us
  blocking collectives  136 us (51%)
  other arithmetic  70.5 us (26%)
  local copies, waits for them, and re-layouts  41.2 us (15%)
  matrix products  12.9 us (5%)
  starting transfers between devices  5.76 us (2%)
    all_to_all x1, blocking collectives, shards(): lax.all_to_all(stacked, 'freq', split_axis=3, concat_axis=3, tiled=True)  59.2 us
    all_to_all x1, blocking collectives, shards(): lax.all_to_all(energy, 'freq', split_axis=2, concat_axis=2, tiled=True)  49 us
    all_gather x1, blocking collectives, shards(): strain = lax.all_gather(strain_spectrum, 'tmpl', axis=2, tiled=True)  27.4 us
    unnamed x13, local copies, waits for them, and re-layouts  21.6 us
    sin x1, other arithmetic, circle(): return (jnp.cos(angles), jnp.sin(angles))  17.6 us
    neg x1, other arithmetic, rotation(): low_half = jnp.concatenate([-sine_table, cosine_table], axis=1)  16.5 us
    convert_element_type x1, other arithmetic, rotation(): return jnp.concatenate([top_half, low_half], axis=0).astype(jnp.bfloat16)  16 us
    dot_general x1, matrix products, shards(): jnp.einsum('tcasb,csad->tbd', shaped, backward, preferred_element_type=jn...  8.34 us
  transfers between devices with their start and end apart: 2, of which 1 were waited for; matrix products, arithmetic and copies ran while one was open for 0% of the time, Pallas kernels for 0%

commit v1 on v0

v1 whole, which is shorter than its diff:
```python
import functools
import math

import jax
import jax.numpy as jnp
from jax import lax
from jax.experimental import pallas as pl
from jax.experimental.pallas import tpu as pltpu
from jax.sharding import PartitionSpec as P

WIN = 256
LANES = 128
CHUNK = 256
HALO = 16
MESH = pl.DeviceIdType.MESH


def unit_circle(index, bits):
    shift = bits - 2
    quarter = (index + (1 << (shift - 1))) >> shift
    rest = index - (quarter << shift)
    angle = rest.astype(jnp.float32) * (2.0 * math.pi / (1 << bits))
    square = angle * angle
    sine = angle * (
        1.0 + square * (-1.0 / 6 + square * (1.0 / 120 + square * (-1.0 / 5040 + square * (1.0 / 362880))))
    )
    cosine = 1.0 + square * (
        -0.5 + square * (1.0 / 24 + square * (-1.0 / 720 + square * (1.0 / 40320 + square * (-1.0 / 3628800))))
    )
    odd = (quarter & 1) == 1
    cos_value = jnp.where(odd, sine, cosine)
    sin_value = jnp.where(odd, cosine, sine)
    cos_value = jnp.where(((quarter + 1) & 2) == 2, -cos_value, cos_value)
    sin_value = jnp.where((quarter & 2) == 2, -sin_value, sin_value)
    return cos_value, sin_value


def iotas(shape):
    return lax.broadcasted_iota(jnp.int32, shape, 0), lax.broadcasted_iota(jnp.int32, shape, 1)


def kernel(
    dims,
    strain_ref,
    bank_ref,
    out_ref,
    bank,
    near_c,
    near_s,
    far_c,
    far_s,
    cos_table,
    sin_table,
    turn_c,
    turn_s,
    packed,
    gathered,
    strain_re,
    strain_im,
    product,
    turned,
    spectra,
    energy,
    series,
    halo,
    result,
    bank_sem,
    out_sem,
    strain_send,
    strain_recv,
    turned_send,
    turned_recv,
    energy_send,
    energy_recv,
    halo_send,
    halo_recv,
):
    groups, members, rows, columns, steps, halves, blocks = dims
    bits = columns.bit_length() - 1
    height = rows * groups
    f = lax.axis_index("freq")
    t = lax.axis_index("tmpl")
    flipped = t + 2 - 4 * ((t // 2) % 2)
    my_half = f // blocks
    my_block = f % blocks

    def partner(j):
        return ((f // 4 + j // 4) % 4) * 4 + (f % 4 + j % 4) % 4

    barrier = pltpu.get_barrier_semaphore()

    def greet(j, carry):
        pl.semaphore_signal(barrier, inc=1, device_id=(f, (t + j) % members), device_id_type=MESH)
        pl.semaphore_signal(barrier, inc=1, device_id=(partner(j), flipped), device_id_type=MESH)
        return carry

    lax.fori_loop(1, groups, greet, 0)

    bank_copy = pltpu.make_async_copy(bank_ref, bank, bank_sem)
    bank_copy.start()
    packed[...] = jnp.concatenate([strain_ref[0], strain_ref[1]], axis=1)

    row, col = iotas((rows, columns))
    near_c[...], near_s[...] = unit_circle((row * col) & (columns - 1), bits)
    row, col = iotas((groups, columns))
    far_c[...], far_s[...] = unit_circle((row * col * rows) & (columns - 1), bits)

    def table(h, carry):
        fc = far_c[pl.ds(h, 1), :]
        fs = far_s[pl.ds(h, 1), :]
        nc = near_c[...]
        ns = near_s[...]
        at = pl.ds(pl.multiple_of(h * rows, rows), rows)
        cos_table[at, :] = (nc * fc - ns * fs).astype(jnp.bfloat16)
        sin_table[at, :] = (ns * fc + nc * fs).astype(jnp.bfloat16)
        return carry

    lax.fori_loop(0, groups, table, 0)

    pl.semaphore_wait(barrier, 2 * (groups - 1))

    def send_strain(j, carry):
        pltpu.make_async_remote_copy(
            src_ref=packed,
            dst_ref=gathered.at[t],
            send_sem=strain_send,
            recv_sem=strain_recv,
            device_id=(f, (t + j) % members),
            device_id_type=MESH,
        ).start()
        return carry

    lax.fori_loop(1, members, send_strain, 0)
    gathered[t] = packed[...]

    row, col = iotas((rows, columns))
    turn_c[...], turn_s[...] = unit_circle((f * rows + row) * col, 2 * bits)

    others = gathered.at[pl.ds(0, members - 1)]
    pltpu.make_async_copy(others, others, strain_recv).wait()
    lane = lax.broadcasted_iota(jnp.int32, (rows, LANES), 1)
    low = lane < LANES // 2
    for pair in range(members // 2):
        first = gathered[2 * pair]
        second = gathered[2 * pair + 1]
        at = pl.ds(pair * LANES, LANES)
        strain_re[:, at] = jnp.where(low, first, pltpu.roll(second, LANES // 2, 1))
        strain_im[:, at] = jnp.where(low, pltpu.roll(first, LANES // 2, 1), second)
    bank_copy.wait()

    def first_pass(i, carry):
        sr = strain_re[...]
        si = strain_im[...]
        for h in range(halves):
            hr = bank[h * steps + i, 0].astype(jnp.float32)
            hi = bank[h * steps + i, 1].astype(jnp.float32)
            product[pl.ds(h * rows, rows), :] = (sr * hr + si * hi).astype(jnp.bfloat16)
            product[pl.ds((halves + h) * rows, rows), :] = (si * hr - sr * hi).astype(jnp.bfloat16)

        def columns_of(n, inner):
            at = pl.ds(pl.multiple_of(n * CHUNK, CHUNK), CHUNK)
            with_cos = jnp.dot(product[...], cos_table[:, at], preferred_element_type=jnp.float32)
            with_sin = jnp.dot(product[...], sin_table[:, at], preferred_element_type=jnp.float32)
            tc = turn_c[:, at]
            ts = turn_s[:, at]
            for h in range(halves):
                up = slice(h * rows, (h + 1) * rows)
                down = slice((halves + h) * rows, (halves + h + 1) * rows)
                re = with_cos[up] - with_sin[down]
                im = with_sin[up] + with_cos[down]
                turned_re = (re * tc - im * ts).astype(jnp.bfloat16)
                turned_im = (re * ts + im * tc).astype(jnp.bfloat16)
                for q in range(CHUNK // LANES):
                    piece = slice(q * LANES, (q + 1) * LANES)
                    d = h * blocks + n * (CHUNK // LANES) + q
                    turned[i, d, :, :LANES] = turned_re[:, piece]
                    turned[i, d, :, LANES:] = turned_im[:, piece]
            return inner

        lax.fori_loop(0, columns // CHUNK, columns_of, 0)

        def send(j, inner):
            d = partner(j)
            pltpu.make_async_remote_copy(
                src_ref=turned.at[i, d],
                dst_ref=spectra.at[i, pl.ds(pl.multiple_of(f * rows, rows), rows)],
                send_sem=turned_send.at[i],
                recv_sem=turned_recv.at[i],
                device_id=(d, flipped),
                device_id_type=MESH,
            ).start()
            return inner

        lax.fori_loop(0, groups, send, 0)
        return carry

    lax.fori_loop(0, steps, first_pass, 0)

    def second_pass(i, carry):
        here = spectra.at[i]
        pltpu.make_async_copy(here, here, turned_recv.at[i]).wait()

        def rows_of(n, inner):
            at = pl.ds(pl.multiple_of(n * CHUNK, CHUNK), CHUNK)
            with_cos = jnp.dot(cos_table[at, :], spectra[i], preferred_element_type=jnp.float32)
            with_sin = jnp.dot(sin_table[at, :], spectra[i], preferred_element_type=jnp.float32)
            re = with_cos[:, :LANES] - with_sin[:, LANES:]
            im = with_sin[:, :LANES] + with_cos[:, LANES:]
            energy[i, at, :] = (re * re + im * im).astype(jnp.bfloat16)
            return inner

        lax.fori_loop(0, height // CHUNK, rows_of, 0)

        def send(j, inner):
            d = partner(j)
            pltpu.make_async_remote_copy(
                src_ref=energy.at[i, pl.ds(pl.multiple_of(d * rows, rows), rows)],
                dst_ref=series.at[i, f],
                send_sem=energy_send.at[i],
                recv_sem=energy_recv.at[i],
                device_id=(d, flipped),
                device_id_type=MESH,
            ).start()

            @pl.when(my_block == blocks - 1)
            def _():
                start = pl.multiple_of((d * rows + height - HALO) % height, HALO)
                pltpu.make_async_remote_copy(
                    src_ref=energy.at[i, pl.ds(start, HALO)],
                    dst_ref=halo.at[i, my_half, 0],
                    send_sem=halo_send.at[i],
                    recv_sem=halo_recv.at[i],
                    device_id=(d, flipped),
                    device_id_type=MESH,
                ).start()

            @pl.when(my_block == 0)
            def _():
                start = pl.multiple_of(((d + 1) * rows) % height, HALO)
                pltpu.make_async_remote_copy(
                    src_ref=energy.at[i, pl.ds(start, HALO)],
                    dst_ref=halo.at[i, my_half, 1],
                    send_sem=halo_send.at[i],
                    recv_sem=halo_recv.at[i],
                    device_id=(d, flipped),
                    device_id_type=MESH,
                ).start()

            return inner

        lax.fori_loop(0, groups, send, 0)
        return carry

    lax.fori_loop(0, steps, second_pass, 0)

    def window(i, carry):
        here = series.at[i]
        pltpu.make_async_copy(here, here, energy_recv.at[i]).wait()
        edges = halo.at[i]
        pltpu.make_async_copy(edges, edges, halo_recv.at[i]).wait()

        def one(h, inner):
            before = halo[i, h, 0].astype(jnp.float32)[HALO - 8 :]
            after = halo[i, h, 1].astype(jnp.float32)[:8]
            tiles = [series[i, h * blocks + b].astype(jnp.float32) for b in range(blocks)]
            follow = jnp.concatenate([after, tiles[0], after], axis=0)
            follow = pltpu.roll(follow, rows + 15, 0)[: rows + 8]
            tiles = [jnp.concatenate([before, tile], axis=0) for tile in tiles] + [follow]
            place = lax.broadcasted_iota(jnp.int32, (rows + 8, LANES), 1)
            stride = 1
            while stride < LANES:
                moved = [pltpu.roll(tile, LANES - stride, 1) for tile in tiles]
                inside = place < LANES - stride
                tiles = [
                    jnp.maximum(tiles[b], jnp.where(inside, moved[b], moved[b + 1])) for b in range(blocks)
                ] + [jnp.maximum(tiles[blocks], moved[blocks])]
                stride *= 2
            ahead = pltpu.roll(tiles[blocks - 1], 1, 0)[8:]
            for b in range(blocks):
                peak = jnp.maximum(ahead, tiles[b][8:])
                ahead = tiles[b][8:]
                result[pl.ds(b * 8 + h * steps + i, rows, stride=8 * blocks), :] = peak
            return inner

        lax.fori_loop(0, halves, one, 0)
        return carry

    lax.fori_loop(0, steps, window, 0)

    out_copy = pltpu.make_async_copy(result, out_ref, out_sem)
    out_copy.start()
    pltpu.make_async_copy(others, others, strain_send).wait()

    def drain(i, carry):
        sent = turned.at[i]
        pltpu.make_async_copy(sent, sent, turned_send.at[i]).wait()
        sent = series.at[i]
        pltpu.make_async_copy(sent, sent, energy_send.at[i]).wait()

        @pl.when((my_block == 0) | (my_block == blocks - 1))
        def _():
            edge = energy.at[i, pl.ds(0, groups * HALO)]
            pltpu.make_async_copy(edge, edge, halo_send.at[i]).wait()

        return carry

    lax.fori_loop(0, steps, drain, 0)
    out_copy.wait()


def shards(groups, members, strain_spectrum, bank_spectra):
    templates, _, rows, columns = bank_spectra.shape
    blocks = columns // LANES
    halves = groups // blocks
    steps = templates // halves
    height = rows * groups
    dims = (groups, members, rows, columns, steps, halves, blocks)
    f32, bf16 = jnp.float32, jnp.bfloat16
    dma = pltpu.SemaphoreType.DMA
    out = pl.pallas_call(
        functools.partial(kernel, dims),
        out_shape=jax.ShapeDtypeStruct((rows * blocks * templates, LANES), f32),
        in_specs=[pl.BlockSpec(memory_space=pltpu.VMEM), pl.BlockSpec(memory_space=pl.ANY)],
        out_specs=pl.BlockSpec(memory_space=pl.ANY),
        scratch_shapes=[
            pltpu.VMEM((templates, 2, rows, columns), bf16),
            pltpu.VMEM((rows, columns), f32),
            pltpu.VMEM((rows, columns), f32),
            pltpu.VMEM((groups, columns), f32),
            pltpu.VMEM((groups, columns), f32),
            pltpu.VMEM((columns, columns), bf16),
            pltpu.VMEM((columns, columns), bf16),
            pltpu.VMEM((rows, columns), f32),
            pltpu.VMEM((rows, columns), f32),
            pltpu.VMEM((rows, LANES), f32),
            pltpu.VMEM((members, rows, LANES), f32),
            pltpu.VMEM((rows, columns), f32),
            pltpu.VMEM((rows, columns), f32),
            pltpu.VMEM((2 * halves * rows, columns), bf16),
            pltpu.VMEM((steps, groups, rows, 2 * LANES), bf16),
            pltpu.VMEM((steps, height, 2 * LANES), bf16),
            pltpu.VMEM((steps, height, LANES), bf16),
            pltpu.VMEM((steps, groups, rows, LANES), bf16),
            pltpu.VMEM((steps, halves, 2, HALO, LANES), bf16),
            pltpu.VMEM((rows * blocks * templates, LANES), f32),
            dma,
            dma,
            dma,
            dma,
            dma((steps,)),
            dma((steps,)),
            dma((steps,)),
            dma((steps,)),
            dma((steps,)),
            dma((steps,)),
        ],
        compiler_params=pltpu.CompilerParams(
            collective_id=0, has_side_effects=True, vmem_limit_bytes=40 * 2**20
        ),
    )(strain_spectrum, bank_spectra)
    out = out.reshape(rows * blocks, templates, LANES).transpose(1, 0, 2)
    return out.reshape(templates, rows * columns)


def solution(mesh):
    body = functools.partial(shards, mesh.shape["freq"], mesh.shape["tmpl"])
    in_specs = (P(None, "freq", "tmpl"), P("tmpl", None, "freq", None))
    return jax.shard_map(body, mesh=mesh, in_specs=in_specs, out_specs=P("tmpl", "freq"), check_vma=False)
```

time: 269 us -> 100 us (0.37)
  blocking collectives: 136 us -> 0 us
  Pallas kernels: 0 us -> 96.2 us
  other arithmetic: 70.5 us -> 0 us
  local copies, waits for them, and re-layouts: 41.2 us -> 3.75 us
  matrix products: 12.9 us -> 0 us
  starting transfers between devices: 5.76 us -> 0 us
    all_to_all x2 -> x0, blocking collectives: 108 us -> none  [the longest x1 59.2 us: shards(): lax.all_to_all(stacked, 'freq', split_axis=3, concat_axis=3, tiled=True)]
    pallas_call x0 -> x1, Pallas kernels: none -> 96.2 us  [shards(): pl.pallas_call(functools.partial(kernel, dims), out_shape=jax.ShapeDtypeS...]
    all_gather x1 -> x0, blocking collectives: 27.4 us -> none  [shards(): strain = lax.all_gather(strain_spectrum, 'tmpl', axis=2, tiled=True)]
    convert_element_type x2 -> x0, other arithmetic: 20 us -> none  [the longest x1 16 us: rotation(): return jnp.concatenate([top_half, low_half], axis=0).astype(jnp.bfloat16)]
    unnamed x13 -> x5, local copies, waits for them, and re-layouts: 21.6 us -> 3.75 us
    sin x1 -> x0, other arithmetic: 17.6 us -> none  [circle(): return (jnp.cos(angles), jnp.sin(angles))]
    neg x1 -> x0, other arithmetic: 16.5 us -> none  [rotation(): low_half = jnp.concatenate([-sine_table, cosine_table], axis=1)]
    dot_general x2 -> x0, matrix products: 12.9 us -> none  [the longest x1 8.34 us: shards(): jnp.einsum('tcasb,csad->tbd', shaped, backward, preferred_element_type=jn...]
  transfers between devices with their start and end apart: 2 -> 0, of which waited for: 1 -> 0; matrix products, arithmetic and copies ran while one was open for 0% -> 0% of each run, Pallas kernels for 0% -> 0%
where the time goes in v1:
time: 100 us
  Pallas kernels  96.2 us (96%)
  local copies, waits for them, and re-layouts  3.75 us (4%)
    pallas_call x1, Pallas kernels, shards(): pl.pallas_call(functools.partial(kernel, dims), out_shape=jax.ShapeDtypeS...  96.2 us
    unnamed x5, local copies, waits for them, and re-layouts  3.75 us

profile of v1, /device:TPU:1, one launch (start us, length us, event | category | flops | bytes accessed | tf_op | source)
XLA Modules:
  0.0 100.0 jit_solution(10789711924887807622)
XLA Ops:
  0.0 0.0 copy-start
  0.0 1.6 %copy-done = bf16[8,2,64,1024]{3,2,1,0:T(8,128)(2,1)S(1)} copy-done((bf16[8,2,64,1024]{3,2,1,0:T(8,128)(2,1)S(1)}, bf16[8,2,64,1024]{3,2,1,0:T(8,128)(2,1)}, u32[]{:S(2)}) %copy-start) | copy-done | bytes 2097176
  1.6 0.0 copy-start.1
  1.6 0.8 copy-done.1
  2.4 96.2 %shard_map.28 = f32[4096,128]{1,0:T(8,128)S(1)} custom-call(f32[2,64,64]{2,1,0:T(8,128)S(1)} %copy-done.1, bf16[8,2,64,1024]{3,2,1,0:T(8,128)(2,1)S(1)} %copy-done), custom_call_target="tpu_custom_call" | custom-call | tf_op jit(solution)/shard_map/pallas_call | solution.py:320
  98.6 1.3 %copy.4 = f32[8,65536]{1,0:T(8,128)} copy(f32[8,65536]{1,0:T(8,128)S(1)} %bitcast.5) | data formatting | bytes 4194304
Async XLA Ops:
  0.0 1.6 %copy-start = (bf16[8,2,64,1024]{3,2,1,0:T(8,128)(2,1)S(1)}, bf16[8,2,64,1024]{3,2,1,0:T(8,128)(2,1)}, u32[]{:S(2)}) copy-start(bf16[8,2,64,1024]{3,2,1,0:T(8,128)(2,1)} %bank_ref.1) | copy-start | bytes 6291460
  1.6 0.8 copy-start.1

commit v2 on v1

--- a/solution.py
+++ b/solution.py
@@ -8,7 +8,6 @@
 from jax.experimental.pallas import tpu as pltpu
 from jax.sharding import PartitionSpec as P
 
-WIN = 256
 LANES = 128
 CHUNK = 256
 HALO = 16
@@ -43,7 +42,8 @@
     dims,
     strain_ref,
     bank_ref,
-    out_ref,
+    result,
+    strain,
     bank,
     near_c,
     near_s,
@@ -63,11 +63,11 @@
     energy,
     series,
     halo,
-    result,
+    strain_sem,
     bank_sem,
-    out_sem,
     strain_send,
     strain_recv,
+    sibling_recv,
     turned_send,
     turned_recv,
     energy_send,
@@ -81,24 +81,33 @@
     f = lax.axis_index("freq")
     t = lax.axis_index("tmpl")
     flipped = t + 2 - 4 * ((t // 2) % 2)
+    sibling = t + 1 - 2 * (t % 2)
+    pairs = members // 2
+    slot = (t % 2) * pairs + t // 2
     my_half = f // blocks
     my_block = f % blocks
 
     def partner(j):
         return ((f // 4 + j // 4) % 4) * 4 + (f % 4 + j % 4) % 4
 
+    strain_copy = pltpu.make_async_copy(strain_ref, strain, strain_sem)
+    strain_copy.start()
     barrier = pltpu.get_barrier_semaphore()
 
-    def greet(j, carry):
-        pl.semaphore_signal(barrier, inc=1, device_id=(f, (t + j) % members), device_id_type=MESH)
+    def greet_partner(j, carry):
         pl.semaphore_signal(barrier, inc=1, device_id=(partner(j), flipped), device_id_type=MESH)
         return carry
 
-    lax.fori_loop(1, groups, greet, 0)
+    def greet_member(j, carry):
+        pl.semaphore_signal(barrier, inc=1, device_id=(f, (t + 2 * j) % members), device_id_type=MESH)
+        return carry
+
+    lax.fori_loop(1, groups, greet_partner, 0)
+    lax.fori_loop(1, pairs, greet_member, 0)
+    pl.semaphore_signal(barrier, inc=1, device_id=(f, sibling), device_id_type=MESH)
 
     bank_copy = pltpu.make_async_copy(bank_ref, bank, bank_sem)
     bank_copy.start()
-    packed[...] = jnp.concatenate([strain_ref[0], strain_ref[1]], axis=1)
 
     row, col = iotas((rows, columns))
     near_c[...], near_s[...] = unit_circle((row * col) & (columns - 1), bits)
@@ -115,34 +124,62 @@
         sin_table[at, :] = (ns * fc + nc * fs).astype(jnp.bfloat16)
         return carry
 
-    lax.fori_loop(0, groups, table, 0)
-
-    pl.semaphore_wait(barrier, 2 * (groups - 1))
+    strain_copy.wait()
+    packed[...] = jnp.concatenate([strain[0], strain[1]], axis=1)
+    pl.semaphore_wait(barrier, groups - 1 + pairs)
 
     def send_strain(j, carry):
         pltpu.make_async_remote_copy(
             src_ref=packed,
-            dst_ref=gathered.at[t],
+            dst_ref=gathered.at[slot],
             send_sem=strain_send,
-            recv_sem=strain_recv,
-            device_id=(f, (t + j) % members),
+            recv_sem=strain_recv.at[j],
+            device_id=(f, (t + 2 * j) % members),
             device_id_type=MESH,
         ).start()
         return carry
 
-    lax.fori_loop(1, members, send_strain, 0)
-    gathered[t] = packed[...]
+    lax.fori_loop(1, pairs, send_strain, 0)
+    pltpu.make_async_remote_copy(
+        src_ref=packed,
+        dst_ref=gathered.at[slot],
+        send_sem=strain_send,
+        recv_sem=sibling_recv,
+        device_id=(f, sibling),
+        device_id_type=MESH,
+    ).start()
+    gathered[slot] = packed[...]
+    per_pair = groups // pairs
+    lax.fori_loop(0, per_pair, table, 0)
+
+    def forward(j, carry):
+        lax.fori_loop(per_pair * j, per_pair * (j + 1), table, 0)
+        source = (t - 2 * j + members) % members
+        block = gathered.at[(t % 2) * pairs + source // 2]
+        pltpu.make_async_copy(block, block, strain_recv.at[j]).wait()
+        pltpu.make_async_remote_copy(
+            src_ref=block,
+            dst_ref=block,
+            send_sem=strain_send,
+            recv_sem=sibling_recv,
+            device_id=(f, sibling),
+            device_id_type=MESH,
+        ).start()
+        return carry
+
+    lax.fori_loop(1, pairs, forward, 0)
 
     row, col = iotas((rows, columns))
     turn_c[...], turn_s[...] = unit_circle((f * rows + row) * col, 2 * bits)
 
-    others = gathered.at[pl.ds(0, members - 1)]
-    pltpu.make_async_copy(others, others, strain_recv).wait()
+    sent = gathered.at[pl.ds(0, members - 1)]
+    half = gathered.at[pl.ds(pl.multiple_of((1 - t % 2) * pairs, pairs), pairs)]
+    pltpu.make_async_copy(half, half, sibling_recv).wait()
     lane = lax.broadcasted_iota(jnp.int32, (rows, LANES), 1)
     low = lane < LANES // 2
     for pair in range(members // 2):
-        first = gathered[2 * pair]
-        second = gathered[2 * pair + 1]
+        first = gathered[pair]
+        second = gathered[pairs + pair]
         at = pl.ds(pair * LANES, LANES)
         strain_re[:, at] = jnp.where(low, first, pltpu.roll(second, LANES // 2, 1))
         strain_im[:, at] = jnp.where(low, pltpu.roll(first, LANES // 2, 1), second)
@@ -157,7 +194,8 @@
             product[pl.ds(h * rows, rows), :] = (sr * hr + si * hi).astype(jnp.bfloat16)
             product[pl.ds((halves + h) * rows, rows), :] = (si * hr - sr * hi).astype(jnp.bfloat16)
 
-        def columns_of(n, inner):
+        def columns_of(j, inner):
+            n = (my_block // 2 + j) % (columns // CHUNK)
             at = pl.ds(pl.multiple_of(n * CHUNK, CHUNK), CHUNK)
             with_cos = jnp.dot(product[...], cos_table[:, at], preferred_element_type=jnp.float32)
             with_sin = jnp.dot(product[...], sin_table[:, at], preferred_element_type=jnp.float32)
@@ -175,23 +213,20 @@
                     d = h * blocks + n * (CHUNK // LANES) + q
                     turned[i, d, :, :LANES] = turned_re[:, piece]
                     turned[i, d, :, LANES:] = turned_im[:, piece]
+            for h in range(halves):
+                for q in range(CHUNK // LANES):
+                    d = h * blocks + n * (CHUNK // LANES) + q
+                    pltpu.make_async_remote_copy(
+                        src_ref=turned.at[i, d],
+                        dst_ref=spectra.at[i, pl.ds(pl.multiple_of(f * rows, rows), rows)],
+                        send_sem=turned_send.at[i],
+                        recv_sem=turned_recv.at[i],
+                        device_id=(d, flipped),
+                        device_id_type=MESH,
+                    ).start()
             return inner
 
         lax.fori_loop(0, columns // CHUNK, columns_of, 0)
-
-        def send(j, inner):
-            d = partner(j)
-            pltpu.make_async_remote_copy(
-                src_ref=turned.at[i, d],
-                dst_ref=spectra.at[i, pl.ds(pl.multiple_of(f * rows, rows), rows)],
-                send_sem=turned_send.at[i],
-                recv_sem=turned_recv.at[i],
-                device_id=(d, flipped),
-                device_id_type=MESH,
-            ).start()
-            return inner
-
-        lax.fori_loop(0, groups, send, 0)
         return carry
 
     lax.fori_loop(0, steps, first_pass, 0)
@@ -287,15 +322,13 @@
 
     lax.fori_loop(0, steps, window, 0)
 
-    out_copy = pltpu.make_async_copy(result, out_ref, out_sem)
-    out_copy.start()
-    pltpu.make_async_copy(others, others, strain_send).wait()
+    pltpu.make_async_copy(sent, sent, strain_send).wait()
 
     def drain(i, carry):
-        sent = turned.at[i]
-        pltpu.make_async_copy(sent, sent, turned_send.at[i]).wait()
-        sent = series.at[i]
-        pltpu.make_async_copy(sent, sent, energy_send.at[i]).wait()
+        out = turned.at[i]
+        pltpu.make_async_copy(out, out, turned_send.at[i]).wait()
+        out = series.at[i]
+        pltpu.make_async_copy(out, out, energy_send.at[i]).wait()
 
         @pl.when((my_block == 0) | (my_block == blocks - 1))
         def _():
@@ -305,7 +338,6 @@
         return carry
 
     lax.fori_loop(0, steps, drain, 0)
-    out_copy.wait()
 
 
 def shards(groups, members, strain_spectrum, bank_spectra):
@@ -320,9 +352,10 @@
     out = pl.pallas_call(
         functools.partial(kernel, dims),
         out_shape=jax.ShapeDtypeStruct((rows * blocks * templates, LANES), f32),
-        in_specs=[pl.BlockSpec(memory_space=pltpu.VMEM), pl.BlockSpec(memory_space=pl.ANY)],
-        out_specs=pl.BlockSpec(memory_space=pl.ANY),
+        in_specs=[pl.BlockSpec(memory_space=pltpu.HBM)] * 2,
+        out_specs=pl.BlockSpec(memory_space=pltpu.VMEM),
         scratch_shapes=[
+            pltpu.VMEM((2, rows, columns // members), f32),
             pltpu.VMEM((templates, 2, rows, columns), bf16),
             pltpu.VMEM((rows, columns), f32),
             pltpu.VMEM((rows, columns), f32),
@@ -342,10 +375,10 @@
             pltpu.VMEM((steps, height, LANES), bf16),
             pltpu.VMEM((steps, groups, rows, LANES), bf16),
             pltpu.VMEM((steps, halves, 2, HALO, LANES), bf16),
-            pltpu.VMEM((rows * blocks * templates, LANES), f32),
             dma,
             dma,
             dma,
+            dma((members // 2,)),
             dma,
             dma((steps,)),
             dma((steps,)),
@@ -357,7 +390,7 @@
         compiler_params=pltpu.CompilerParams(
             collective_id=0, has_side_effects=True, vmem_limit_bytes=40 * 2**20
         ),
-    )(strain_spectrum, bank_spectra)
+    )(*[pltpu.with_memory_space_constraint(x, pltpu.HBM) for x in (strain_spectrum, bank_spectra)])
     out = out.reshape(rows * blocks, templates, LANES).transpose(1, 0, 2)
     return out.reshape(templates, rows * columns)
 

time: 100 us -> 95.9 us (0.959)
  local copies, waits for them, and re-layouts: 3.75 us -> 1.32 us
  Pallas kernels: 96.2 us -> 94.4 us
    unnamed x5 -> x1, local copies, waits for them, and re-layouts: 3.75 us -> 1.32 us
    pallas_call x1, Pallas kernels: 96.2 us -> 94.4 us  [shards(): pl.pallas_call(functools.partial(kernel, dims), out_shape=jax.ShapeDtypeS...]
where the time goes in v2:
time: 95.9 us; the launch traced here: 95.8 us
  Pallas kernels  94.4 us (98%)
  local copies, waits for them, and re-layouts  1.32 us (1%)
    pallas_call x1, Pallas kernels, shards(): pl.pallas_call(functools.partial(kernel, dims), out_shape=jax.ShapeDtypeS...  94.4 us

profile of v2, /device:TPU:1, one launch (start us, length us, event | category | flops | bytes accessed | tf_op | source)
XLA Modules:
  0.0 95.8 jit_solution(14171763391250217993)
XLA Ops:
  0.0 94.4 %shard_map.28 = f32[4096,128]{1,0:T(8,128)S(1)} custom-call(f32[2,64,64]{2,1,0:T(8,128)} %strain_ref.1, bf16[8,2,64,1024]{3,2,1,0:T(8,128)(2,1)} %bank_ref.1), custom_call_target="tpu_custom_call" | custom-call | tf_op jit(solution)/shard_map/pallas_call | solution.py:352
  94.4 1.3 %copy.4 = f32[8,65536]{1,0:T(8,128)} copy(f32[8,65536]{1,0:T(8,128)S(1)} %bitcast.5) | data formatting | bytes 4194304

commit v3 on v2

--- a/solution.py
+++ b/solution.py
@@ -10,7 +10,6 @@
 
 LANES = 128
 CHUNK = 256
-HALO = 16
 MESH = pl.DeviceIdType.MESH
 
 
@@ -62,6 +61,7 @@
     spectra,
     energy,
     series,
+    edges,
     halo,
     strain_sem,
     bank_sem,
@@ -241,7 +241,12 @@
             with_sin = jnp.dot(sin_table[at, :], spectra[i], preferred_element_type=jnp.float32)
             re = with_cos[:, :LANES] - with_sin[:, LANES:]
             im = with_sin[:, :LANES] + with_cos[:, LANES:]
-            energy[i, at, :] = (re * re + im * im).astype(jnp.bfloat16)
+            power = re * re + im * im
+            energy[i, at, :] = power.astype(jnp.bfloat16)
+            for q in range(CHUNK // rows):
+                top = power[q * rows : q * rows + 1]
+                bottom = power[(q + 1) * rows - 1 : (q + 1) * rows]
+                edges[i, n * (CHUNK // rows) + q] = jnp.where(my_block == 0, top, bottom)
             return inner
 
         lax.fori_loop(0, height // CHUNK, rows_of, 0)
@@ -257,30 +262,18 @@
                 device_id_type=MESH,
             ).start()
 
-            @pl.when(my_block == blocks - 1)
+            @pl.when((my_block == 0) | (my_block == blocks - 1))
             def _():
-                start = pl.multiple_of((d * rows + height - HALO) % height, HALO)
+                side = 1 - my_block // (blocks - 1)
                 pltpu.make_async_remote_copy(
-                    src_ref=energy.at[i, pl.ds(start, HALO)],
-                    dst_ref=halo.at[i, my_half, 0],
+                    src_ref=edges.at[i, (d + groups - 1 + 2 * side) % groups],
+                    dst_ref=halo.at[i, my_half, side],
                     send_sem=halo_send.at[i],
                     recv_sem=halo_recv.at[i],
                     device_id=(d, flipped),
                     device_id_type=MESH,
                 ).start()
 
-            @pl.when(my_block == 0)
-            def _():
-                start = pl.multiple_of(((d + 1) * rows) % height, HALO)
-                pltpu.make_async_remote_copy(
-                    src_ref=energy.at[i, pl.ds(start, HALO)],
-                    dst_ref=halo.at[i, my_half, 1],
-                    send_sem=halo_send.at[i],
-                    recv_sem=halo_recv.at[i],
-                    device_id=(d, flipped),
-                    device_id_type=MESH,
-                ).start()
-
             return inner
 
         lax.fori_loop(0, groups, send, 0)
@@ -291,12 +284,12 @@
     def window(i, carry):
         here = series.at[i]
         pltpu.make_async_copy(here, here, energy_recv.at[i]).wait()
-        edges = halo.at[i]
-        pltpu.make_async_copy(edges, edges, halo_recv.at[i]).wait()
+        outer = halo.at[i]
+        pltpu.make_async_copy(outer, outer, halo_recv.at[i]).wait()
 
         def one(h, inner):
-            before = halo[i, h, 0].astype(jnp.float32)[HALO - 8 :]
-            after = halo[i, h, 1].astype(jnp.float32)[:8]
+            before = jnp.broadcast_to(halo[i, h, 0], (8, LANES))
+            after = jnp.broadcast_to(halo[i, h, 1], (8, LANES))
             tiles = [series[i, h * blocks + b].astype(jnp.float32) for b in range(blocks)]
             follow = jnp.concatenate([after, tiles[0], after], axis=0)
             follow = pltpu.roll(follow, rows + 15, 0)[: rows + 8]
@@ -332,7 +325,7 @@
 
         @pl.when((my_block == 0) | (my_block == blocks - 1))
         def _():
-            edge = energy.at[i, pl.ds(0, groups * HALO)]
+            edge = edges.at[i]
             pltpu.make_async_copy(edge, edge, halo_send.at[i]).wait()
 
         return carry
@@ -374,7 +367,8 @@
             pltpu.VMEM((steps, height, 2 * LANES), bf16),
             pltpu.VMEM((steps, height, LANES), bf16),
             pltpu.VMEM((steps, groups, rows, LANES), bf16),
-            pltpu.VMEM((steps, halves, 2, HALO, LANES), bf16),
+            pltpu.VMEM((steps, groups, 1, LANES), f32),
+            pltpu.VMEM((steps, halves, 2, 1, LANES), f32),
             dma,
             dma,
             dma,

time: 95.9 us -> 92.2 us (0.961)
  Pallas kernels: 94.4 us -> 90.8 us
    pallas_call x1, Pallas kernels: 94.4 us -> 90.8 us  [shards(): pl.pallas_call(functools.partial(kernel, dims), out_shape=jax.ShapeDtypeS...]
where the time goes in v3:
time: 92.2 us; the launch traced here: 92.1 us
  Pallas kernels  90.8 us (98%)
  local copies, waits for them, and re-layouts  1.32 us (1%)
    pallas_call x1, Pallas kernels, shards(): pl.pallas_call(functools.partial(kernel, dims), out_shape=jax.ShapeDtypeS...  90.8 us

profile of v3, /device:TPU:1, one launch (start us, length us, event | category | flops | bytes accessed | tf_op | source)
XLA Modules:
  0.0 92.1 jit_solution(7321377779860168254)
XLA Ops:
  0.0 90.8 %shard_map.28 = f32[4096,128]{1,0:T(8,128)S(1)} custom-call(f32[2,64,64]{2,1,0:T(8,128)} %strain_ref.1, bf16[8,2,64,1024]{3,2,1,0:T(8,128)(2,1)} %bank_ref.1), custom_call_target="tpu_custom_call" | custom-call | tf_op jit(solution)/shard_map/pallas_call | solution.py:345
  90.8 1.3 %copy.4 = f32[8,65536]{1,0:T(8,128)} copy(f32[8,65536]{1,0:T(8,128)S(1)} %bitcast.5) | data formatting | bytes 4194304
